TPU v7x, 256 devices: a whole 4x4x8 slice. The times are simulated.
256 devices in a mesh: row: 2 (over core), sector: 32 (over z, y), slab: 4 (over x).
Axes of the slice: x: 4, y: 4, z: 8, core: 2. Of those that a mesh axis runs over, the one named last changes fastest.
Arguments:
- state: float32 [2, 5, 32, 1024, 128], P('row', None, 'slab', 'sector'), may hold values from -6 to 6
- source: float32 [2, 5, 32, 1024, 128], P('row', None, 'slab', 'sector'), may hold values from -6 to 6
- diag_inverse: float32 [2, 5, 5, 32, 1024, 128], P('row', None, None, 'slab', 'sector'), may hold values from -1 to 1
- jac_axial: float32 [2, 5, 5], P('row'), may hold values from -1 to 2
- jac_cross: float32 [2, 2, 5, 5], P('row'), may hold values from -2.5 to 2.5
- owner: int32 [1024], replicated, may hold values from 0 to 1023, as said below
Outputs:
- residual: float32 [2, 5, 32, 1024, 128], P('row', None, 'slab', 'sector')
- new_state: float32 [2, 5, 32, 1024, 128], P('row', None, 'slab', 'sector')
Inputs may be any that keep to these rules, and one draw needn't show every extreme that they name: owner is a permutation; for some whole s, the columns b * 32 to b * 32 + 31 of the rotor face exactly the stator columns s + b * 32 to s + b * 32 + 31, taken modulo 1024, for every b.
All inputs are finite; a program needn't handle non-finite values.
Results may differ from a plain program's by a relative error of at most 0.0001.
Values sent between devices are 32-bit elements; how exact they have to be, the bound alone decides.
No kernel may reach another device: no remote copies, remote signals or barrier semaphores. Data moves between devices by JAX's collectives and lax.ppermute only.
A program may use at most 64 MiB of HBM per device.

v0:
```python
import jax
import jax.numpy as jnp
from jax import lax
from jax.experimental import pallas as pl
from jax.experimental.pallas import tpu as pltpu
from jax.sharding import PartitionSpec as P

F32 = jnp.float32
V = 5
AXES = ("row", "sector", "slab")
VMEM_BYTES = 14 * 1024 * 1024


def matvec(mat, vec):
    out = []
    for i in range(V):
        acc = mat(i, 0) * vec[0]
        for j in range(1, V):
            acc = acc + mat(i, j) * vec[j]
        out.append(acc)
    return out


def stacked(ref, base):
    return lambda i, j: ref[base + V * i + j]


def planes_of(ref, base):
    return [ref[base + v] for v in range(V)]


def put(ref, base, values):
    for v in range(V):
        ref[base + v] = values[v]


def sliding(owner, columns, total):
    lead = owner[0]

    def lower(i, best):
        return jnp.minimum(best, ((owner[i] - lead + total // 2) & (total - 1)) - total // 2)

    return (lead + lax.fori_loop(1, columns, lower, jnp.int32(0), unroll=True)) & (total - 1)


def pack_kernel(
    planes, columns, state, towards_low, interface, towards_high, lowest,
):
    row = lax.axis_index("row")
    face = jnp.where(row == 0, planes - 1, 0)
    for v in range(V):
        plane = state[0, v, face]
        interface[v] = plane
        towards_low[v, planes:] = plane
        lowest[v] = state[0, v, 0]
        for x in range(planes):
            towards_low[v, x : x + 1] = state[0, v, x, 0:1]
            towards_high[v, x : x + 1] = state[0, v, x, columns - 1 : columns]


def load_kernel(inverse, lowest, blocks, arrived):
    copy = pltpu.make_async_copy(inverse, blocks, arrived)
    copy.start()
    copy.wait()


def halved(ref, which=0):
    entries = [
        [jnp.broadcast_to(0.5 * ref[i, which : which + 1, j : j + 1], (8, 128)) for j in range(V)]
        for i in range(V)
    ]
    return lambda i, j: entries[i][j]


def window_kernel(planes, columns, sectors, owner, own, next_one, next_two, message, pair, table, landing):
    row = lax.axis_index("row")
    sector = lax.axis_index("sector")
    total = sectors * columns
    for v in range(V):
        table[v, 0:columns] = own[v]
        table[v, columns : 2 * columns] = next_one[v, planes:]
        table[v, 2 * columns :] = next_two[v]
    turn = sliding(owner, columns, total) >> (columns.bit_length() - 1)
    even = turn & -2
    pair[0] = turn >> 1

    @pl.when(row == 1)
    def _():
        facing = (sector - even) & (sectors - 1)

        def step(i, carry):
            at = (owner[facing * columns + i] - sector * columns) & (total - 1)
            at = jnp.minimum(at, 3 * columns - 1)
            for v in range(V):
                landing[v, pl.ds(i, 1)] = table[v, pl.ds(at, 1)]
            return carry

        lax.fori_loop(0, columns, step, 0, unroll=8)

    @pl.when(row == 0)
    def _():
        facing = (sector + even + 2) & (sectors - 1)
        first = (1 - (turn - even)) * columns

        def step(i, carry):
            at = first + i
            column = owner[(sector * columns + at) & (total - 1)]
            to = jnp.minimum((column - facing * columns) & (total - 1), columns)
            for v in range(V):
                landing[v, pl.ds(to, 1)] = table[v, pl.ds(at, 1)]
            return carry

        lax.fori_loop(0, 2 * columns, step, 0, unroll=8)

    for v in range(V):
        message[v] = landing[v, 0:columns]


def matrix_kernel(
    planes, axial, inverse, prefix_out, right, left, product, prefix, left_now, right_now,
):
    row = lax.axis_index("row")
    slab = lax.axis_index("slab")
    scaled = halved(axial)

    def one_strip(step, carry):
        at = pl.ds(pl.multiple_of(step * 8, 8), 8)

        def factor(x):
            return lambda i, j: product[x, V * i + j]

        def flux_times(x):
            for i in range(V):
                entries = [inverse[0, i, k, x, at] for k in range(V)]
                for j in range(V):
                    acc = entries[0] * scaled(0, j)
                    for k in range(1, V):
                        acc = acc + entries[k] * scaled(k, j)
                    product[x, V * i + j] = acc

        def forward(x, carry):
            flux_times(x)
            for j in range(V):
                column = [prefix[x - 1, V * i + j] for i in range(V)]
                put_column(prefix.at[x], j, matvec(factor(x), column))
            return carry

        flux_times(0)
        for k in range(V * V):
            prefix[0, k] = product[0, k]
        lax.fori_loop(1, planes, forward, 0)
        for k in range(V * V):
            prefix_out[k, at] = prefix[planes - 1, k]

        @pl.when(slab > 0)
        def _():
            for j in range(V):
                column = [prefix[planes - 2, V * i + j] for i in range(V)]
                put_column(left_now, j, matvec(factor(planes - 1), column))

            def backward(step, carry):
                x = planes - 1 - step
                for j in range(V):
                    column = [prefix[x - 1, V * i + j] - left_now[V * i + j] for i in range(V)]
                    put_column(left_now, j, matvec(factor(x), column))
                return carry

            lax.fori_loop(1, planes - 1, backward, 0)
            for j in range(V):
                column = [float(i == j) - left_now[V * i + j] for i in range(V)]
                put_column(left_now, j, matvec(factor(0), column))
            for k in range(V * V):
                left[k, at] = left_now[k]

        @pl.when((slab == 1) | (slab == 2) | ((slab == 3) & (row == 0)))
        def _():
            for k in range(V * V):
                right_now[k] = product[planes - 1, k]

            def backward(step, carry):
                x = planes - 1 - step
                for j in range(V):
                    column = [right_now[V * i + j] for i in range(V)]
                    put_column(right_now, j, matvec(factor(x), column))
                return carry

            lax.fori_loop(1, planes, backward, 0)
            for k in range(V * V):
                right[k, at] = right_now[k]

        return carry

    lax.fori_loop(0, inverse.shape[4] // 8, one_strip, 0)


def put_column(ref, j, values):
    for i in range(V):
        ref[V * i + j] = values[i]


def residual_kernel(
    planes, columns, axial, cross, state, source, inverse, from_high, from_low, above, prefix_in,
    residual, up, down, wide, forward,
):
    for v in range(V):
        for x in range(planes):
            wide[v, x, 8 : 8 + columns] = state[0, v, x]
            wide[v, x, 7:8] = from_low[v, x : x + 1]
            wide[v, x, 8 + columns : 9 + columns] = from_high[v, x : x + 1]
    rows = lax.broadcasted_iota(jnp.int32, (8, 128), 0)
    lanes = lax.broadcasted_iota(jnp.int32, (8, 128), 1)
    ja = halved(axial)
    jb = halved(cross)
    jr = halved(cross, 1)

    def one_strip(step, carry):
        at = pl.ds(pl.multiple_of(step * 8, 8), 8)
        middle = pl.ds(pl.multiple_of(step * 8 + 8, 8), 8)
        high = pl.ds(pl.multiple_of(step * 8 + 16, 8), 8)
        previous = None
        for x in range(planes):
            along, around, outward = [], [], []
            for v in range(V):
                here = wide[v, x, middle]
                nearer = wide[v, x + 1, middle] if x + 1 < planes else above[v, at]
                along.append(nearer - wide[v, x - 1, middle] if x else nearer)
                plus = jnp.where(rows == 0, wide[v, x, high], here)
                minus = jnp.where(rows == 7, wide[v, x, at], here)
                around.append(pltpu.roll(plus, 7, 0) - pltpu.roll(minus, 1, 0))
                outward.append(
                    jnp.where(lanes == 127, 0.0, pltpu.roll(here, 127, 1))
                    - jnp.where(lanes == 0, 0.0, pltpu.roll(here, 1, 1))
                )
            one, two, three = matvec(ja, along), matvec(jb, around), matvec(jr, outward)
            values = [source[0, v, x, at] - (one[v] + two[v] + three[v]) for v in range(V)]
            for v in range(V):
                residual[v, x, at] = values[v]
            if previous is not None:
                carried = matvec(ja, previous)
                values = [values[v] + carried[v] for v in range(V)]
            previous = matvec(lambda i, j: inverse[0, i, j, x, at], values)
            for v in range(V):
                forward[v, x] = previous[v]
        for v in range(V):
            last = wide[v, planes - 1, middle]
            up[v, at] = previous[v] + last
        for k in range(V * V):
            up[V + k, at] = prefix_in[k, at]
        for v in range(V):
            up[V + V * V + v, at] = wide[v, planes - 1, middle]
        for x in range(planes - 2, -1, -1):
            carried = matvec(lambda i, j: inverse[0, i, j, x, at], matvec(ja, previous))
            previous = [forward[v, x] - carried[v] for v in range(V)]
        for v in range(V):
            down[v, at] = previous[v]
        return carry

    lax.fori_loop(0, columns // 8, one_strip, 0)


def first_kernel(ghost, up, down, right, left, entry, onward, packed):
    slab = lax.axis_index("slab")

    @pl.when(slab == 0)
    def _():
        moved = matvec(stacked(up, V), planes_of(ghost, 0))
        leaving = [up[v] + moved[v] for v in range(V)]
        put(entry, 0, leaving)
        put(onward, 0, leaving)
        put(onward, V, planes_of(up, V + V * V))

    @pl.when(slab == 3)
    def _():
        packed[V:] = left[...]
        moved = matvec(stacked(right, 0), planes_of(ghost, 0))
        for v in range(V):
            packed[v] = jnp.where(lax.axis_index("row") == 0, down[v] + moved[v], down[v])


def lower_kernel(to_one, begun, right, lower):
    @pl.when(lax.axis_index("slab") == 1)
    def _():
        moved = matvec(stacked(right, 0), planes_of(to_one, 0))
        put(lower, 0, [begun[v] + moved[v] for v in range(V)])


def middle_kernel(came, came_side, up_other, side_other, up, down, right, left, lower, third, second, top):
    slab = lax.axis_index("slab")

    @pl.when(slab == 1)
    def _():
        moved = matvec(stacked(left, 0), planes_of(came_side, 0))
        put(lower, 0, [down[v] + moved[v] for v in range(V)])

    @pl.when(slab == 2)
    def _():
        moved = matvec(stacked(up_other, V), planes_of(came, 0))
        inflow = [up_other[v] + moved[v] for v in range(V)]
        moved = matvec(stacked(up, V), inflow)
        onward = [up[v] + moved[v] for v in range(V)]
        moved = matvec(stacked(side_other, V), onward)
        beyond = [side_other[v] + moved[v] for v in range(V)]
        moved = matvec(stacked(left, 0), inflow)
        again = matvec(stacked(right, 0), beyond)
        put(lower, 0, [down[v] + moved[v] + again[v] for v in range(V)])
        put(third, 0, onward)
        put(third, V, planes_of(up, V + V * V))
        put(second, 0, inflow)
        put(top, 0, beyond)


def last_kernel(
    planes, axial, ghost, up_other, came_side, to_third, to_zero, to_one, second, top,
    partial, inverse, state, residual, new_state, forward, inflow, beyond, under,
):
    row = lax.axis_index("row")
    slab = lax.axis_index("slab")
    ja = halved(axial)
    has_top = jnp.where((row == 0) & (slab == 3), 1.0, 0.0)

    at = pl.ds(pl.multiple_of(pl.program_id(0) * 8, 8), 8)

    def fetch(ref, base=0):
        return [ref[base + v, at] for v in range(V)]

    @pl.when(slab == 0)
    def _():
        put(inflow, 0, fetch(ghost))
        put(under, 0, fetch(ghost))
        put(beyond, 0, fetch(to_zero))

    @pl.when(slab == 1)
    def _():
        put(inflow, 0, fetch(came_side))
        put(under, 0, fetch(came_side, V))
        put(beyond, 0, fetch(to_one))

    @pl.when(slab == 2)
    def _():
        put(inflow, 0, fetch(second))
        put(under, 0, fetch(up_other, V + V * V))
        put(beyond, 0, fetch(top))

    @pl.when(slab == 3)
    def _():
        put(inflow, 0, fetch(to_third))
        put(under, 0, fetch(to_third, V))
        put(beyond, 0, [jnp.zeros((8, 128), F32)] * V)

    previous = planes_of(inflow, 0)
    for x in range(planes):
        values = [partial[v, x, at] for v in range(V)]
        if x == planes - 1:
            top_part = matvec(ja, [ghost[v, at] * has_top for v in range(V)])
            values = [values[v] - top_part[v] for v in range(V)]
        if x == 0:
            bottom = matvec(ja, planes_of(under, 0))
            for v in range(V):
                residual[0, v, x] = values[v] + bottom[v]
        else:
            for v in range(V):
                residual[0, v, x] = values[v]
        carried = matvec(ja, previous)
        values = [values[v] + carried[v] for v in range(V)]
        previous = matvec(lambda i, j: inverse[0, i, j, x, at], values)
        for v in range(V):
            forward[v, x] = previous[v]
    following = planes_of(beyond, 0)
    for x in range(planes - 1, -1, -1):
        carried = matvec(lambda i, j: inverse[0, i, j, x, at], matvec(ja, following))
        following = [forward[v, x] - carried[v] for v in range(V)]
        for v in range(V):
            new_state[0, v, x] = state[0, v, x, at] + following[v]


def near(*shape):
    return pltpu.VMEM(shape, F32)


def sds(*shape):
    return jax.ShapeDtypeStruct(shape, F32)


SCALARS = pl.BlockSpec(memory_space=pltpu.SMEM)
WHOLE = pl.BlockSpec(memory_space=pltpu.VMEM)


def params(**more):
    return pltpu.CompilerParams(vmem_limit_bytes=VMEM_BYTES, **more)


def cost(amount):
    return pl.CostEstimate(flops=amount, bytes_accessed=amount // 8, transcendentals=0)


def per_device(state, source, diag_inverse, jac_axial, jac_cross, owner):
    planes, columns, radial = state.shape[2:]
    sectors = lax.axis_size("sector")
    slabs = lax.axis_size("slab")
    plane = (V, columns, radial)
    cells = pl.BlockSpec((1, V, planes, 8, radial), lambda i: (0, 0, 0, i, 0))
    size = slabs * sectors

    def device(row, sector, slab):
        return row * size + sector % sectors * slabs + slab

    def import_pairs(even):
        pairs = []
        for j in range(sectors):
            pairs.append((device(1, j, 0), device(0, j - even, slabs - 1)))
            pairs.append((device(0, j, slabs - 1), device(1, j + even + 2, 0)))
        return pairs

    two_down = []
    for j in range(sectors):
        two_down.append((device(0, j, slabs - 1), device(0, j - 2, slabs - 1)))
        two_down.append((device(1, j, 0), device(1, j - 2, 0)))

    total = sectors * columns
    assert total & (total - 1) == 0 and columns & (columns - 1) == 0
    axial = jnp.transpose(jac_axial, (1, 0, 2))
    cross = jnp.transpose(jac_cross[0], (1, 0, 2))
    towards_low, interface, towards_high, lowest = pl.pallas_call(
        lambda *refs: pack_kernel(planes, columns, *refs),
        out_shape=(near(V, planes + columns, radial), near(*plane), near(V, planes, radial), near(*plane)),
        compiler_params=params(),
        name="pack",
    )(state)
    above = lax.ppermute(lowest, "slab", [(k, k - 1) for k in range(1, slabs)])
    from_low = lax.ppermute(towards_high, "sector", [(j, (j + 1) % sectors) for j in range(sectors)])
    from_second = lax.ppermute(interface, AXES, two_down)
    from_high = lax.ppermute(towards_low, "sector", [(j, (j - 1) % sectors) for j in range(sectors)])

    square = near(V * V, columns, radial)
    blocks = pl.pallas_call(
        load_kernel,
        in_specs=[pl.BlockSpec(memory_space=pltpu.HBM), pl.BlockSpec(memory_space=pl.ANY)],
        out_specs=WHOLE,
        out_shape=near(*diag_inverse.shape),
        scratch_shapes=[pltpu.SemaphoreType.DMA],
        compiler_params=params(),
        cost_estimate=cost(20_000_000),
        name="load",
    )(pltpu.with_memory_space_constraint(diag_inverse, pltpu.HBM), lowest)
    message, pair = pl.pallas_call(
        lambda *refs: window_kernel(planes, columns, sectors, *refs),
        in_specs=[SCALARS] + [WHOLE] * 3,
        out_specs=[WHOLE, SCALARS],
        out_shape=(near(*plane), jax.ShapeDtypeStruct((1,), jnp.int32)),
        scratch_shapes=[
            pltpu.VMEM((V, 3 * columns, radial), F32),
            pltpu.VMEM((V, columns + 8, radial), F32),
        ],
        compiler_params=params(),
        name="window",
    )(owner, interface, from_high, from_second)

    def exchange(even, message, from_low, above, from_high, blocks):
        ghost = lax.ppermute(message, AXES, import_pairs(even))
        prefix, right, left = pl.pallas_call(
            lambda *refs: matrix_kernel(planes, *refs),
            in_specs=[WHOLE, WHOLE],
            out_shape=(square, square, square),
            scratch_shapes=[
                pltpu.VMEM((planes, V * V, 8, radial), F32),
                pltpu.VMEM((planes, V * V, 8, radial), F32),
                pltpu.VMEM((V * V, 8, radial), F32),
                pltpu.VMEM((V * V, 8, radial), F32),
            ],
            compiler_params=params(),
            cost_estimate=cost(60_000_000),
            name="matrices",
        )(axial, blocks)
        partial, up, down = pl.pallas_call(
            lambda *refs: residual_kernel(planes, columns, *refs),
            in_specs=[WHOLE] * 9,
            out_shape=(
                near(V, planes, columns, radial), near(2 * V + V * V, columns, radial), near(*plane),
            ),
            scratch_shapes=[
                pltpu.VMEM((V, planes, columns + 16, radial), F32),
                pltpu.VMEM((V, planes, 8, radial), F32),
            ],
            compiler_params=params(),
            cost_estimate=cost(40_000_000),
            name="residual",
        )(axial, cross, state, source, blocks, from_high, from_low, above, prefix)
        return ghost, partial, up, down, right, left

    ghost, partial, up, down, right, left = lax.switch(
        pair[0],
        [lambda *args, e=e: exchange(2 * e, *args) for e in range(sectors // 2)],
        message, from_low, above, from_high, blocks,
    )
    up_other = lax.ppermute(up, "slab", [(1, 2)])
    entry, side_message, packed = pl.pallas_call(
        first_kernel,
        out_shape=(near(*plane), near(2 * V, columns, radial), near(V + V * V, columns, radial)),
        compiler_params=params(),
        name="first",
    )(ghost, up, down, right, left)
    side_other = lax.ppermute(packed, "slab", [(3, 2)])
    came = lax.ppermute(entry, "slab", [(0, 2)])
    side_message, came = lax.optimization_barrier((side_message, came))
    came_side = lax.ppermute(side_message, "slab", [(0, 1)])
    lower, onward, second, top = pl.pallas_call(
        middle_kernel,
        out_shape=(near(*plane), near(2 * V, columns, radial), near(*plane), near(*plane)),
        compiler_params=params(),
        name="middle",
    )(came, came_side, up_other, side_other, up, down, right, left)
    to_one = lax.ppermute(lower, "slab", [(2, 1)])
    onward, arrived = lax.optimization_barrier((onward, to_one))
    to_third = lax.ppermute(onward, "slab", [(2, 3)])
    lowest_update = pl.pallas_call(
        lower_kernel,
        out_shape=near(*plane),
        compiler_params=params(),
        name="lower",
    )(to_one, lower, right)
    to_zero = lax.ppermute(lowest_update, "slab", [(1, 0)])

    residual, new_state = pl.pallas_call(
        lambda *refs: last_kernel(planes, *refs),
        grid=(columns // 8,),
        in_specs=[WHOLE] * 12,
        out_specs=(cells, cells),
        out_shape=(sds(*state.shape), sds(*state.shape)),
        scratch_shapes=[pltpu.VMEM((V, planes, 8, radial), F32)] + [pltpu.VMEM((V, 8, radial), F32)] * 3,
        compiler_params=params(),
        name="last",
    )(
        axial, ghost, up_other, came_side, to_third, to_zero, arrived, second, top,
        partial, blocks, state,
    )
    return residual, new_state


def solution(mesh):
    return jax.shard_map(
        per_device,
        mesh=mesh,
        in_specs=(
            P("row", None, "slab", "sector", None),
            P("row", None, "slab", "sector", None),
            P("row", None, None, "slab", "sector", None),
            P("row", None, None),
            P("row", None, None, None),
            P(),
        ),
        out_specs=(P("row", None, "slab", "sector", None), P("row", None, "slab", "sector", None)),
        check_vma=False,
    )
```

profile of v0, /device:TPU:0, one launch (start us, length us, event | category | flops | bytes accessed | tf_op | source)
XLA Modules:
  0.0 62.2 jit_solution(16244446608791777830)
XLA Ops:
  0.6 1.1 %pack.1 = (f32[5,40,128]{2,1,0:T(8,128)S(1)}, f32[5,32,128]{2,1,0:T(8,128)S(1)}, f32[5,8,128]{2,1,0:T(8,128)S(1)}, f32[5,32,128]{2,1,0:T(8,128)S(1)}) custom-call(f32[1,5,8,32,128]{4,3,2,1,0:T(8,128)} %refs_11_.1), custom_call_target="tpu_custom_call" | custom-call | tf_op jit(solution)/shard_map/pack/pallas_call | solution.py:423
  1.8 6.6 %collective-permute-start.16 = (f32[5,40,128]{2,1,0:T(8,128)S(1)}, f32[5,40,128]{2,1,0:T(8,128)S(1)}, u32[]{:S(2)}, u32[]{:S(2)}) collective-permute-start(f32[5,40,128]{2,1,0:T(8,128)S(1)} %get-tuple-element.554), channel_id=1, source_target_pairs={{0,124},{4,0},{8,4},{12,8},{16,12},{20,16},{24,20},{28,24},{32,28}... | collective-permute-start | bytes 307208 | tf_op jit(solution)/shard_map/ppermute | solution.py:432
  8.4 0.7 %collective-permute-start.17 = (f32[5,32,128]{2,1,0:T(8,128)S(1)}, f32[5,32,128]{2,1,0:T(8,128)S(1)}, u32[]{:S(2)}, u32[]{:S(2)}) collective-permute-start(f32[5,32,128]{2,1,0:T(8,128)S(1)} %get-tuple-element.553.refs_1_), channel_id=1, source_target_pairs={{3,123},{128,248},{7,127},{132,252},{11,3},{136,128},{15,7},{140,1... | collective-permute-start | bytes 245768 | tf_op jit(solution)/shard_map/ppermute | solution.py:431
  9.1 1.3 %collective-permute-start.19 = (f32[5,32,128]{2,1,0:T(8,128)S(1)}, f32[5,32,128]{2,1,0:T(8,128)S(1)}, u32[]{:S(2)}, u32[]{:S(2)}) collective-permute-start(f32[5,32,128]{2,1,0:T(8,128)S(1)} %get-tuple-element.557.lowest), channel_id=1, source_target_pairs={{1,0},{2,1},{3,2},{5,4},{6,5},{7,6},{9,8},{10,9},{11,10},{13,12},{... | collective-permute-start | bytes 245768 | tf_op jit(solution)/shard_map/ppermute | solution.py:429
  10.4 0.0 copy-start.17
  10.4 0.0 copy-start.18
  10.4 0.0 copy-start.20
  10.4 0.0 copy-start.21
  10.4 0.0 copy-start.22
  10.4 0.1 collective-permute-start.18
  10.5 2.0 %load.1.refs_10_ = f32[1,5,5,8,32,128]{5,4,3,2,1,0:T(8,128)S(1)} custom-call(f32[1,5,5,8,32,128]{5,4,3,2,1,0:T(8,128)} %inverse.1, f32[5,32,128]{2,1,0:T(8,128)S(1)} %get-tuple-element.557.lowest), custom_call_target="tpu_custom_call" | custom-call | flops 20000000 | bytes 2500000 | tf_op jit(solution)/shard_map/load/pallas_call | solution.py:435
  12.5 0.0 collective-permute-done.17.refs_3_
  12.6 0.0 collective-permute-done.16.refs_2_
  12.6 0.0 copy-done.17
  12.6 1.4 %window.1 = (f32[5,32,128]{2,1,0:T(8,128)S(1)}, s32[1]{0:T(128)}) custom-call(s32[1024]{0:T(1024)S(1)} %copy-done.17, f32[5,32,128]{2,1,0:T(8,128)S(1)} %get-tuple-element.553.refs_1_, f32[5,40,128]{2,1,0:T(8,128)S(1)} %collective-permute-done.16.refs_2_, f32[5,32,128]{2,1,0:T(8,128)S(1)} %collective-permute-done.17.refs_3_), custom_call_target="tpu_custom_call" | custom-call | tf_op jit(solution)/shard_map/window/pallas_call | solution.py:445
  14.7 3.0 %collective-permute-done.18 = f32[5,8,128]{2,1,0:T(8,128)S(1)} collective-permute-done((f32[5,8,128]{2,1,0:T(8,128)S(1)}, f32[5,8,128]{2,1,0:T(8,128)S(1)}, u32[]{:S(2)}, u32[]{:S(2)}) %collective-permute-start.18) | collective-permute-done | bytes 20512 | tf_op jit(solution)/shard_map/ppermute | solution.py:430
  17.7 0.0 collective-permute-done.19
  17.7 0.0 copy-done.18
  17.7 0.0 copy-done.20
  17.7 0.0 copy-done.21
  17.7 0.0 copy-done.22
  17.7 7.6 %conditional.1 = (f32[5,32,128]{2,1,0:T(8,128)}, f32[5,8,32,128]{3,2,1,0:T(8,128)}, f32[35,32,128]{2,1,0:T(8,128)S(1)}, f32[5,32,128]{2,1,0:T(8,128)S(1)}, f32[2...) conditional(s32[]{:T(128)} %bitcast.1, (f32[5,32,128]{2,1,0:T(8,128)S(1)}, ...), branch_computations={%region_0.0_spmd, %region_1.0_spmd, %region_2.0_spmd, %region_3.0_... | conditional | flops 100000000 | bytes 15449236 | solution.py:490
  17.7 1.3 %collective-permute-start = (f32[5,32,128]{2,1,0:T(8,128)S(1)}, f32[5,32,128]{2,1,0:T(8,128)}, u32[]{:S(2)}, u32[]{:S(2)}) collective-permute-start(f32[5,32,128]{2,1,0:T(8,128)S(1)} %get-tuple-element.288), channel_id=1, source_target_pairs={{128,3},{3,136},{132,7},{7,140},{136,11},{11,144},{140,15},{15,148... | collective-permute-start | bytes 245768 | tf_op jit(solution)/shard_map/cond/branch_0_fun/ppermute | solution.py:459
  19.0 3.4 %matrices.16 = (f32[25,32,128]{2,1,0:T(8,128)S(1)}, f32[25,32,128]{2,1,0:T(8,128)S(1)}, f32[25,32,128]{2,1,0:T(8,128)}) custom-call(f32[5,1,5]{2,1,0:T(1,128)S(1)} %get-tuple-element.289.refs_0_, f32[1,5,5,8,32,128]{5,4,3,2,1,0:T(8,128)S(1)} %get-tuple-element.293.refs_1_.refs_4_), custom_call_target="tpu_custom_call" | custom-call | flops 60000000 | bytes 7500000 | tf_op jit(solution)/shard_map/cond/branch_0_fun/matrices/pallas_call | solution.py:460
  22.4 2.1 %residual.16 = (f32[5,8,32,128]{3,2,1,0:T(8,128)S(1)}, f32[35,32,128]{2,1,0:T(8,128)S(1)}, f32[5,32,128]{2,1,0:T(8,128)S(1)}) custom-call(f32[5,1,5]{2,1,0:T(1,128)S(1)} %get-tuple-element.289.refs_0_, f32[5,2,5]{2,1,0:T(2,128)S(1)} %get-tuple-element.290.refs_1_, f32[1,5,8,32,128]{4,3,2,1,0:T(8,128)S(1)} %get-tuple-element.291.refs_2_, ...), custom_call_target="tpu_custom_call" | custom-call | flops 40000000 | bytes 5000000 | tf_op jit(solution)/shard_map/cond/branch_0_fun/residual/pallas_call | solution.py:474
  24.4 0.0 copy-start
  24.5 0.0 collective-permute-done
  24.5 0.8 %copy-done = f32[5,8,32,128]{3,2,1,0:T(8,128)} copy-done((f32[5,8,32,128]{3,2,1,0:T(8,128)}, f32[5,8,32,128]{3,2,1,0:T(8,128)S(1)}, u32[]{:S(2)}) %copy-start) | copy-done | bytes 655384 | tf_op jit(solution)/shard_map/cond
  25.3 0.0 copy-start.19
  25.3 0.8 %collective-permute-start.20 = (f32[35,32,128]{2,1,0:T(8,128)S(1)}, f32[35,32,128]{2,1,0:T(8,128)S(1)}, u32[]{:S(2)}, u32[]{:S(2)}) collective-permute-start(f32[35,32,128]{2,1,0:T(8,128)S(1)} %get-tuple-element.560.up), channel_id=1, source_target_pairs={{1,2},{5,6},{9,10},{13,14},{17,18},{21,22},{25,26},{29,30},{33,34}... | collective-permute-start | bytes 1720328 | tf_op jit(solution)/shard_map/ppermute | solution.py:495
  26.1 1.1 %first.1 = (f32[5,32,128]{2,1,0:T(8,128)S(1)}, f32[10,32,128]{2,1,0:T(8,128)S(1)}, f32[30,32,128]{2,1,0:T(8,128)S(1)}) custom-call(f32[5,32,128]{2,1,0:T(8,128)} %get-tuple-element.559.ghost.refs_1_, f32[35,32,128]{2,1,0:T(8,128)S(1)} %get-tuple-element.560.up, f32[5,32,128]{2,1,0:T(8,128)S(1)} %get-tuple-element.561.down, ...), custom_call_target="tpu_custom_call" | custom-call | tf_op jit(solution)/shard_map/first/pallas_call | solution.py:496
  27.2 0.7 %collective-permute-start.23 = (f32[30,32,128]{2,1,0:T(8,128)S(1)}, f32[30,32,128]{2,1,0:T(8,128)S(1)}, u32[]{:S(2)}, u32[]{:S(2)}) collective-permute-start(f32[30,32,128]{2,1,0:T(8,128)S(1)} %get-tuple-element.568), channel_id=1, source_target_pairs={{3,2},{7,6},{11,10},{15,14},{19,18},{23,22},{27,26},{31,30},{35,34... | collective-permute-start | bytes 1474568 | tf_op jit(solution)/shard_map/ppermute | solution.py:502
  27.9 9.5 %collective-permute-start.21 = (f32[5,32,128]{2,1,0:T(8,128)S(1)}, f32[5,32,128]{2,1,0:T(8,128)S(1)}, u32[]{:S(2)}, u32[]{:S(2)}) collective-permute-start(f32[5,32,128]{2,1,0:T(8,128)S(1)} %get-tuple-element.565), channel_id=1, source_target_pairs={{0,2},{4,6},{8,10},{12,14},{16,18},{20,22},{24,26},{28,30},{32,34}... | collective-permute-start | bytes 245768 | tf_op jit(solution)/shard_map/ppermute | solution.py:503
  37.4 2.8 %collective-permute-done.21.came = f32[5,32,128]{2,1,0:T(8,128)S(1)} collective-permute-done((f32[5,32,128]{2,1,0:T(8,128)S(1)}, f32[5,32,128]{2,1,0:T(8,128)S(1)}, u32[]{:S(2)}, u32[]{:S(2)}) %collective-permute-start.21) | collective-permute-done | bytes 81952 | tf_op jit(solution)/shard_map/ppermute | solution.py:503
  40.2 1.3 %collective-permute-start.22 = (f32[10,32,128]{2,1,0:T(8,128)S(1)}, f32[10,32,128]{2,1,0:T(8,128)S(1)}, u32[]{:S(2)}, u32[]{:S(2)}) collective-permute-start(f32[10,32,128]{2,1,0:T(8,128)S(1)} %get-tuple-element.566), channel_id=1, source_target_pairs={{0,1},{4,5},{8,9},{12,13},{16,17},{20,21},{24,25},{28,29},{32,33},... | collective-permute-start | bytes 491528 | tf_op jit(solution)/shard_map/ppermute | solution.py:505
  41.5 2.8 %collective-permute-done.22.came_side.refs_3_ = f32[10,32,128]{2,1,0:T(8,128)S(1)} collective-permute-done((f32[10,32,128]{2,1,0:T(8,128)S(1)}, f32[10,32,128]{2,1,0:T(8,128)S(1)}, u32[]{:S(2)}, u32[]{:S(2)}) %collective-permute-start.22) | collective-permute-done | bytes 163872 | tf_op jit(solution)/shard_map/ppermute | solution.py:505
  44.3 0.0 collective-permute-done.23.side_other
  44.4 0.0 collective-permute-done.20.up_other.refs_2_
  44.4 1.0 %middle.1 = (f32[5,32,128]{2,1,0:T(8,128)S(1)}, f32[10,32,128]{2,1,0:T(8,128)S(1)}, f32[5,32,128]{2,1,0:T(8,128)S(1)}, f32[5,32,128]{2,1,0:T(8,128)S(1)}) custom-call(f32[5,32,128]{2,1,0:T(8,128)S(1)} %collective-permute-done.21.came, f32[10,32,128]{2,1,0:T(8,128)S(1)} %collective-permute-done.22.came_side.refs_3_, ...), custom_call_target="tpu_custom_call" | custom-call | tf_op jit(solution)/shard_map/middle/pallas_call | solution.py:506
  45.4 0.7 %collective-permute-start.24 = (f32[5,32,128]{2,1,0:T(8,128)S(1)}, f32[5,32,128]{2,1,0:T(8,128)S(1)}, u32[]{:S(2)}, u32[]{:S(2)}) collective-permute-start(f32[5,32,128]{2,1,0:T(8,128)S(1)} %get-tuple-element.570.begun), channel_id=1, source_target_pairs={{2,1},{6,5},{10,9},{14,13},{18,17},{22,21},{26,25},{30,29},{34,33}... | collective-permute-start | bytes 245768 | tf_op jit(solution)/shard_map/ppermute | solution.py:512
  46.0 0.0 collective-permute-done.24.to_one.refs_6_
  46.0 0.7 %collective-permute-start.25 = (f32[10,32,128]{2,1,0:T(8,128)S(1)}, f32[10,32,128]{2,1,0:T(8,128)S(1)}, u32[]{:S(2)}, u32[]{:S(2)}) collective-permute-start(f32[10,32,128]{2,1,0:T(8,128)S(1)} %get-tuple-element.571), channel_id=1, source_target_pairs={{2,3},{6,7},{10,11},{14,15},{18,19},{22,23},{26,27},{30,31},{34,35... | collective-permute-start | bytes 491528 | tf_op jit(solution)/shard_map/ppermute | solution.py:514
  46.7 1.3 %collective-permute-start.26 = (f32[5,32,128]{2,1,0:T(8,128)S(1)}, f32[5,32,128]{2,1,0:T(8,128)S(1)}, u32[]{:S(2)}, u32[]{:S(2)}) collective-permute-start(f32[5,32,128]{2,1,0:T(8,128)S(1)} %lower.1), channel_id=1, source_target_pairs={{1,0},{5,4},{9,8},{13,12},{17,16},{21,20},{25,24},{29,28},{33,32},... | collective-permute-start | bytes 245768 | tf_op jit(solution)/shard_map/ppermute | solution.py:521
  48.0 10.6 %collective-permute-done.26.refs_5_ = f32[5,32,128]{2,1,0:T(8,128)S(1)} collective-permute-done((f32[5,32,128]{2,1,0:T(8,128)S(1)}, f32[5,32,128]{2,1,0:T(8,128)S(1)}, u32[]{:S(2)}, u32[]{:S(2)}) %collective-permute-start.26) | collective-permute-done | bytes 81952 | tf_op jit(solution)/shard_map/ppermute | solution.py:521
  58.6 0.0 collective-permute-done.25.refs_4_
  58.6 0.0 copy-done.16
  58.6 0.0 copy-done.19
  58.6 3.5 %last.1 = (f32[1,5,8,32,128]{4,3,2,1,0:T(8,128)}, f32[1,5,8,32,128]{4,3,2,1,0:T(8,128)}) custom-call(f32[5,1,5]{2,1,0:T(1,128)S(1)} %bitcast.21, f32[5,32,128]{2,1,0:T(8,128)} %get-tuple-element.559.ghost.refs_1_, f32[35,32,128]{2,1,0:T(8,128)S(1)} %collective-permute-done.20.up_other.refs_2_, f32[10,32,128]{2,1,0:T(8,128)S(1)} %collective-permute-done.22.came_side.refs_3_, ...), custom_call_target="tpu_custom_call" | custom-call | tf_op jit(solution)/shard_map/last/pallas_call | solution.py:523
  (2 shorter events, 0.0 us)
Async XLA Ops:
  1.8 10.8 %collective-permute-start.16 = (f32[5,40,128]{2,1,0:T(8,128)S(1)}, f32[5,40,128]{2,1,0:T(8,128)S(1)}, u32[]{:S(2)}, u32[]{:S(2)}) collective-permute-start(f32[5,40,128]{2,1,0:T(8,128)S(1)} %get-tuple-element.554), channel_id=1, source_target_pairs={{0,124},{4,0},{8,4},{12,8},{16,12},{20,16},{24,20},{28,24},{32,28}... | collective-permute-start | bytes 307208 | tf_op jit(solution)/shard_map/ppermute | solution.py:432
  8.4 4.1 %collective-permute-start.17 = (f32[5,32,128]{2,1,0:T(8,128)S(1)}, f32[5,32,128]{2,1,0:T(8,128)S(1)}, u32[]{:S(2)}, u32[]{:S(2)}) collective-permute-start(f32[5,32,128]{2,1,0:T(8,128)S(1)} %get-tuple-element.553.refs_1_), channel_id=1, source_target_pairs={{3,123},{128,248},{7,127},{132,252},{11,3},{136,128},{15,7},{140,1... | collective-permute-start | bytes 245768 | tf_op jit(solution)/shard_map/ppermute | solution.py:431
  9.1 8.6 %collective-permute-start.19 = (f32[5,32,128]{2,1,0:T(8,128)S(1)}, f32[5,32,128]{2,1,0:T(8,128)S(1)}, u32[]{:S(2)}, u32[]{:S(2)}) collective-permute-start(f32[5,32,128]{2,1,0:T(8,128)S(1)} %get-tuple-element.557.lowest), channel_id=1, source_target_pairs={{1,0},{2,1},{3,2},{5,4},{6,5},{7,6},{9,8},{10,9},{11,10},{13,12},{... | collective-permute-start | bytes 245768 | tf_op jit(solution)/shard_map/ppermute | solution.py:429
  10.4 2.2 %copy-start.17 = (s32[1024]{0:T(1024)S(1)}, s32[1024]{0:T(1024)}, u32[]{:S(2)}) copy-start(s32[1024]{0:T(1024)} %refs_0_.3) | copy-start | bytes 12292
  10.4 7.3 %copy-start.18 = (f32[1,5,8,32,128]{4,3,2,1,0:T(8,128)S(1)}, f32[1,5,8,32,128]{4,3,2,1,0:T(8,128)}, u32[]{:S(2)}) copy-start(f32[1,5,8,32,128]{4,3,2,1,0:T(8,128)} %refs_11_.1) | copy-start | bytes 1966084
  10.4 7.3 %copy-start.20 = (f32[1,5,8,32,128]{4,3,2,1,0:T(8,128)S(1)}, f32[1,5,8,32,128]{4,3,2,1,0:T(8,128)}, u32[]{:S(2)}) copy-start(f32[1,5,8,32,128]{4,3,2,1,0:T(8,128)} %param.23) | copy-start | bytes 1966084
  10.4 7.3 %copy-start.21 = (f32[1,5,5]{2,0,1:T(1,128)S(1)}, f32[1,5,5]{2,0,1:T(1,128)}, u32[]{:S(2)}) copy-start(f32[1,5,5]{2,0,1:T(1,128)} %param.25) | copy-start | bytes 304
  10.4 7.3 %copy-start.22 = (f32[1,2,5,5]{3,1,2,0:T(2,128)S(1)}, f32[1,2,5,5]{3,1,2,0:T(2,128)}, u32[]{:S(2)}) copy-start(f32[1,2,5,5]{3,1,2,0:T(2,128)} %param.26) | copy-start | bytes 604
  10.4 7.2 %collective-permute-start.18 = (f32[5,8,128]{2,1,0:T(8,128)S(1)}, f32[5,8,128]{2,1,0:T(8,128)S(1)}, u32[]{:S(2)}, u32[]{:S(2)}) collective-permute-start(f32[5,8,128]{2,1,0:T(8,128)S(1)} %get-tuple-element.558), channel_id=1, source_target_pairs={{0,4},{4,8},{8,12},{12,16},{16,20},{20,24},{24,28},{28,32},{32,36}... | collective-permute-start | bytes 61448 | tf_op jit(solution)/shard_map/ppermute | solution.py:430
  17.7 6.7 %collective-permute-start = (f32[5,32,128]{2,1,0:T(8,128)S(1)}, f32[5,32,128]{2,1,0:T(8,128)}, u32[]{:S(2)}, u32[]{:S(2)}) collective-permute-start(f32[5,32,128]{2,1,0:T(8,128)S(1)} %get-tuple-element.288), channel_id=1, source_target_pairs={{128,3},{3,136},{132,7},{7,140},{136,11},{11,144},{140,15},{15,148... | collective-permute-start | bytes 245768 | tf_op jit(solution)/shard_map/cond/branch_0_fun/ppermute | solution.py:459
  24.4 0.8 %copy-start = (f32[5,8,32,128]{3,2,1,0:T(8,128)}, f32[5,8,32,128]{3,2,1,0:T(8,128)S(1)}, u32[]{:S(2)}) copy-start(f32[5,8,32,128]{3,2,1,0:T(8,128)S(1)} %get-tuple-element.577) | copy-start | bytes 1966084 | tf_op jit(solution)/shard_map/cond
  25.3 33.4 %copy-start.16 = (f32[5,8,32,128]{3,2,1,0:T(8,128)S(1)}, f32[5,8,32,128]{3,2,1,0:T(8,128)}, u32[]{:S(2)}) copy-start(f32[5,8,32,128]{3,2,1,0:T(8,128)} %get-tuple-element.575.refs_9_) | copy-start | bytes 1966084
  25.3 33.4 %copy-start.19 = (f32[1,5,8,32,128]{4,3,2,1,0:T(8,128)S(1)}, f32[1,5,8,32,128]{4,3,2,1,0:T(8,128)}, u32[]{:S(2)}) copy-start(f32[1,5,8,32,128]{4,3,2,1,0:T(8,128)} %refs_11_.1) | copy-start | bytes 1966084
  25.3 19.1 %collective-permute-start.20 = (f32[35,32,128]{2,1,0:T(8,128)S(1)}, f32[35,32,128]{2,1,0:T(8,128)S(1)}, u32[]{:S(2)}, u32[]{:S(2)}) collective-permute-start(f32[35,32,128]{2,1,0:T(8,128)S(1)} %get-tuple-element.560.up), channel_id=1, source_target_pairs={{1,2},{5,6},{9,10},{13,14},{17,18},{21,22},{25,26},{29,30},{33,34}... | collective-permute-start | bytes 1720328 | tf_op jit(solution)/shard_map/ppermute | solution.py:495
  27.2 17.1 %collective-permute-start.23 = (f32[30,32,128]{2,1,0:T(8,128)S(1)}, f32[30,32,128]{2,1,0:T(8,128)S(1)}, u32[]{:S(2)}, u32[]{:S(2)}) collective-permute-start(f32[30,32,128]{2,1,0:T(8,128)S(1)} %get-tuple-element.568), channel_id=1, source_target_pairs={{3,2},{7,6},{11,10},{15,14},{19,18},{23,22},{27,26},{31,30},{35,34... | collective-permute-start | bytes 1474568 | tf_op jit(solution)/shard_map/ppermute | solution.py:502
  27.9 12.3 %collective-permute-start.21 = (f32[5,32,128]{2,1,0:T(8,128)S(1)}, f32[5,32,128]{2,1,0:T(8,128)S(1)}, u32[]{:S(2)}, u32[]{:S(2)}) collective-permute-start(f32[5,32,128]{2,1,0:T(8,128)S(1)} %get-tuple-element.565), channel_id=1, source_target_pairs={{0,2},{4,6},{8,10},{12,14},{16,18},{20,22},{24,26},{28,30},{32,34}... | collective-permute-start | bytes 245768 | tf_op jit(solution)/shard_map/ppermute | solution.py:503
  40.2 4.1 %collective-permute-start.22 = (f32[10,32,128]{2,1,0:T(8,128)S(1)}, f32[10,32,128]{2,1,0:T(8,128)S(1)}, u32[]{:S(2)}, u32[]{:S(2)}) collective-permute-start(f32[10,32,128]{2,1,0:T(8,128)S(1)} %get-tuple-element.566), channel_id=1, source_target_pairs={{0,1},{4,5},{8,9},{12,13},{16,17},{20,21},{24,25},{28,29},{32,33},... | collective-permute-start | bytes 491528 | tf_op jit(solution)/shard_map/ppermute | solution.py:505
  45.4 0.7 %collective-permute-start.24 = (f32[5,32,128]{2,1,0:T(8,128)S(1)}, f32[5,32,128]{2,1,0:T(8,128)S(1)}, u32[]{:S(2)}, u32[]{:S(2)}) collective-permute-start(f32[5,32,128]{2,1,0:T(8,128)S(1)} %get-tuple-element.570.begun), channel_id=1, source_target_pairs={{2,1},{6,5},{10,9},{14,13},{18,17},{22,21},{26,25},{30,29},{34,33}... | collective-permute-start | bytes 245768 | tf_op jit(solution)/shard_map/ppermute | solution.py:512
  46.0 12.6 %collective-permute-start.25 = (f32[10,32,128]{2,1,0:T(8,128)S(1)}, f32[10,32,128]{2,1,0:T(8,128)S(1)}, u32[]{:S(2)}, u32[]{:S(2)}) collective-permute-start(f32[10,32,128]{2,1,0:T(8,128)S(1)} %get-tuple-element.571), channel_id=1, source_target_pairs={{2,3},{6,7},{10,11},{14,15},{18,19},{22,23},{26,27},{30,31},{34,35... | collective-permute-start | bytes 491528 | tf_op jit(solution)/shard_map/ppermute | solution.py:514
  46.7 11.9 %collective-permute-start.26 = (f32[5,32,128]{2,1,0:T(8,128)S(1)}, f32[5,32,128]{2,1,0:T(8,128)S(1)}, u32[]{:S(2)}, u32[]{:S(2)}) collective-permute-start(f32[5,32,128]{2,1,0:T(8,128)S(1)} %lower.1), channel_id=1, source_target_pairs={{1,0},{5,4},{9,8},{13,12},{17,16},{21,20},{25,24},{29,28},{33,32},... | collective-permute-start | bytes 245768 | tf_op jit(solution)/shard_map/ppermute | solution.py:521
where the time goes:
time: 62.7 us; the launch traced here: 62.2 us
  starting transfers between devices  24.9 us (40%)
  waiting for transfers between devices  19.2 us (31%)
  Pallas kernels  15.6 us (25%)
  between operations  1.49 us (2%)
  local copies, waits for them, and re-layouts  0.86 us (1%)
    ppermute x1, waiting for transfers between devices, per_device(): to_zero = lax.ppermute(lowest_update, 'slab', [(1, 0)])  10.6 us
    ppermute x1, starting transfers between devices, per_device(): came = lax.ppermute(entry, 'slab', [(0, 2)])  9.52 us
    ppermute x1, starting transfers between devices, per_device(): lax.ppermute(towards_low, 'sector', [(j, (j - 1) % sectors) for j in rang...  6.65 us
    pallas_call x1, Pallas kernels, per_device(): pl.pallas_call(lambda *refs: last_kernel(planes, *refs), grid=(columns //...  3.51 us
    pallas_call x1, Pallas kernels, exchange(): pl.pallas_call(lambda *refs: matrix_kernel(planes, *refs), in_specs=[WHOL...  3.37 us
    ppermute x1, waiting for transfers between devices, per_device(): lax.ppermute(towards_high, 'sector', [(j, (j + 1) % sectors) for j in ran...  2.97 us
    ppermute x1, waiting for transfers between devices, per_device(): came = lax.ppermute(entry, 'slab', [(0, 2)])  2.81 us
    ppermute x1, waiting for transfers between devices, per_device(): came_side = lax.ppermute(side_message, 'slab', [(0, 1)])  2.81 us
  transfers between devices with their start and end apart: 12, of which 4 were waited for; matrix products, arithmetic and copies ran while one was open for 0% of the time, Pallas kernels for 16%

commit v1 on v0

--- a/solution.py
+++ b/solution.py
@@ -277,20 +277,16 @@
             packed[v] = jnp.where(lax.axis_index("row") == 0, down[v] + moved[v], down[v])
 
 
-def lower_kernel(to_one, begun, right, lower):
+def lower_kernel(to_one, came_side, down, right, left, lower):
     @pl.when(lax.axis_index("slab") == 1)
     def _():
-        moved = matvec(stacked(right, 0), planes_of(to_one, 0))
-        put(lower, 0, [begun[v] + moved[v] for v in range(V)])
-
-
-def middle_kernel(came, came_side, up_other, side_other, up, down, right, left, lower, third, second, top):
+        moved = matvec(stacked(left, 0), planes_of(came_side, 0))
+        again = matvec(stacked(right, 0), planes_of(to_one, 0))
+        put(lower, 0, [down[v] + moved[v] + again[v] for v in range(V)])
+
+
+def middle_kernel(came, up_other, side_other, up, down, right, left, lower, third, second, top):
     slab = lax.axis_index("slab")
-
-    @pl.when(slab == 1)
-    def _():
-        moved = matvec(stacked(left, 0), planes_of(came_side, 0))
-        put(lower, 0, [down[v] + moved[v] for v in range(V)])
 
     @pl.when(slab == 2)
     def _():
@@ -508,7 +504,7 @@
         out_shape=(near(*plane), near(2 * V, columns, radial), near(*plane), near(*plane)),
         compiler_params=params(),
         name="middle",
-    )(came, came_side, up_other, side_other, up, down, right, left)
+    )(came, up_other, side_other, up, down, right, left)
     to_one = lax.ppermute(lower, "slab", [(2, 1)])
     onward, arrived = lax.optimization_barrier((onward, to_one))
     to_third = lax.ppermute(onward, "slab", [(2, 3)])
@@ -517,7 +513,7 @@
         out_shape=near(*plane),
         compiler_params=params(),
         name="lower",
-    )(to_one, lower, right)
+    )(to_one, came_side, down, right, left)
     to_zero = lax.ppermute(lowest_update, "slab", [(1, 0)])
 
     residual, new_state = pl.pallas_call(

time: 62.7 us -> 62.7 us (level); the launches traced: 62.2 us -> 61.5 us
  starting transfers between devices: 24.9 us -> 33 us
  waiting for transfers between devices: 19.2 us -> 12.2 us
  Pallas kernels: 15.6 us -> 13.7 us
    ppermute x1, starting transfers between devices: 1.29 us -> 9.41 us  [per_device(): came_side = lax.ppermute(side_message, 'slab', [(0, 1)])]
    ppermute x1, waiting for transfers between devices: 10.6 us -> 5.03 us  [per_device(): to_zero = lax.ppermute(lowest_update, 'slab', [(1, 0)])]
    pallas_call x1, Pallas kernels: 1 us -> 0.01 us  [per_device(): pl.pallas_call(middle_kernel, out_shape=(near(*plane), near(2 * V, column...]
    ppermute x1, waiting for transfers between devices: 2.81 us -> 2.04 us  [per_device(): came = lax.ppermute(entry, 'slab', [(0, 2)])]
    pallas_call x1, Pallas kernels: 3.37 us -> 2.62 us  [exchange(): pl.pallas_call(lambda *refs: matrix_kernel(planes, *refs), in_specs=[WHOL...]
    ppermute x1, waiting for transfers between devices: 2.81 us -> 2.12 us  [per_device(): came_side = lax.ppermute(side_message, 'slab', [(0, 1)])]
  transfers between devices with their start and end apart: 12 -> 12, of which waited for: 4 -> 4; matrix products, arithmetic and copies ran while one was open for 0% -> 0% of each run, Pallas kernels for 16% -> 15%
where the time goes in v1:
time: 62.7 us; the launch traced here: 61.5 us
  starting transfers between devices  33 us (53%)
  Pallas kernels  13.7 us (22%)
  waiting for transfers between devices  12.2 us (19%)
  between operations  1.49 us (2%)
  local copies, waits for them, and re-layouts  0.86 us (1%)
    ppermute x1, starting transfers between devices, per_device(): came = lax.ppermute(entry, 'slab', [(0, 2)])  9.51 us
    ppermute x1, starting transfers between devices, per_device(): came_side = lax.ppermute(side_message, 'slab', [(0, 1)])  9.41 us
    ppermute x1, starting transfers between devices, per_device(): lax.ppermute(towards_low, 'sector', [(j, (j - 1) % sectors) for j in rang...  6.65 us
    ppermute x1, waiting for transfers between devices, per_device(): to_zero = lax.ppermute(lowest_update, 'slab', [(1, 0)])  5.03 us
    pallas_call x1, Pallas kernels, per_device(): pl.pallas_call(lambda *refs: last_kernel(planes, *refs), grid=(columns //...  3.51 us
    ppermute x1, waiting for transfers between devices, per_device(): lax.ppermute(towards_high, 'sector', [(j, (j + 1) % sectors) for j in ran...  2.97 us
    pallas_call x1, Pallas kernels, exchange(): pl.pallas_call(lambda *refs: matrix_kernel(planes, *refs), in_specs=[WHOL...  2.62 us
    ppermute x1, waiting for transfers between devices, per_device(): came_side = lax.ppermute(side_message, 'slab', [(0, 1)])  2.12 us
  transfers between devices with their start and end apart: 12, of which 4 were waited for; matrix products, arithmetic and copies ran while one was open for 0% of the time, Pallas kernels for 15%

profile of v1, /device:TPU:0, one launch (start us, length us, event | category | flops | bytes accessed | tf_op | source)
XLA Modules:
  0.0 61.5 jit_solution(8151042392935973999)
XLA Ops:
  0.6 1.1 %pack.1 = (f32[5,40,128]{2,1,0:T(8,128)S(1)}, f32[5,32,128]{2,1,0:T(8,128)S(1)}, f32[5,8,128]{2,1,0:T(8,128)S(1)}, f32[5,32,128]{2,1,0:T(8,128)S(1)}) custom-call(f32[1,5,8,32,128]{4,3,2,1,0:T(8,128)} %refs_11_.1), custom_call_target="tpu_custom_call" | custom-call | tf_op jit(solution)/shard_map/pack/pallas_call | solution.py:419
  1.8 6.6 %collective-permute-start.16 = (f32[5,40,128]{2,1,0:T(8,128)S(1)}, f32[5,40,128]{2,1,0:T(8,128)S(1)}, u32[]{:S(2)}, u32[]{:S(2)}) collective-permute-start(f32[5,40,128]{2,1,0:T(8,128)S(1)} %get-tuple-element.554), channel_id=1, source_target_pairs={{0,124},{4,0},{8,4},{12,8},{16,12},{20,16},{24,20},{28,24},{32,28}... | collective-permute-start | bytes 307208 | tf_op jit(solution)/shard_map/ppermute | solution.py:428
  8.4 0.7 %collective-permute-start.17 = (f32[5,32,128]{2,1,0:T(8,128)S(1)}, f32[5,32,128]{2,1,0:T(8,128)S(1)}, u32[]{:S(2)}, u32[]{:S(2)}) collective-permute-start(f32[5,32,128]{2,1,0:T(8,128)S(1)} %get-tuple-element.553.refs_1_), channel_id=1, source_target_pairs={{3,123},{128,248},{7,127},{132,252},{11,3},{136,128},{15,7},{140,1... | collective-permute-start | bytes 245768 | tf_op jit(solution)/shard_map/ppermute | solution.py:427
  9.1 1.3 %collective-permute-start.19 = (f32[5,32,128]{2,1,0:T(8,128)S(1)}, f32[5,32,128]{2,1,0:T(8,128)S(1)}, u32[]{:S(2)}, u32[]{:S(2)}) collective-permute-start(f32[5,32,128]{2,1,0:T(8,128)S(1)} %get-tuple-element.557.lowest), channel_id=1, source_target_pairs={{1,0},{2,1},{3,2},{5,4},{6,5},{7,6},{9,8},{10,9},{11,10},{13,12},{... | collective-permute-start | bytes 245768 | tf_op jit(solution)/shard_map/ppermute | solution.py:425
  10.4 0.0 copy-start.17
  10.4 0.0 copy-start.18
  10.4 0.0 copy-start.20
  10.4 0.0 copy-start.21
  10.4 0.0 copy-start.22
  10.4 0.1 collective-permute-start.18
  10.5 2.0 %load.1.refs_10_ = f32[1,5,5,8,32,128]{5,4,3,2,1,0:T(8,128)S(1)} custom-call(f32[1,5,5,8,32,128]{5,4,3,2,1,0:T(8,128)} %inverse.1, f32[5,32,128]{2,1,0:T(8,128)S(1)} %get-tuple-element.557.lowest), custom_call_target="tpu_custom_call" | custom-call | flops 20000000 | bytes 2500000 | tf_op jit(solution)/shard_map/load/pallas_call | solution.py:431
  12.5 0.0 collective-permute-done.17.refs_3_
  12.6 0.0 collective-permute-done.16.refs_2_
  12.6 0.0 copy-done.17
  12.6 1.4 %window.1 = (f32[5,32,128]{2,1,0:T(8,128)S(1)}, s32[1]{0:T(128)}) custom-call(s32[1024]{0:T(1024)S(1)} %copy-done.17, f32[5,32,128]{2,1,0:T(8,128)S(1)} %get-tuple-element.553.refs_1_, f32[5,40,128]{2,1,0:T(8,128)S(1)} %collective-permute-done.16.refs_2_, f32[5,32,128]{2,1,0:T(8,128)S(1)} %collective-permute-done.17.refs_3_), custom_call_target="tpu_custom_call" | custom-call | tf_op jit(solution)/shard_map/window/pallas_call | solution.py:441
  14.7 3.0 %collective-permute-done.18 = f32[5,8,128]{2,1,0:T(8,128)S(1)} collective-permute-done((f32[5,8,128]{2,1,0:T(8,128)S(1)}, f32[5,8,128]{2,1,0:T(8,128)S(1)}, u32[]{:S(2)}, u32[]{:S(2)}) %collective-permute-start.18) | collective-permute-done | bytes 20512 | tf_op jit(solution)/shard_map/ppermute | solution.py:426
  17.7 0.0 collective-permute-done.19
  17.7 0.0 copy-done.18
  17.7 0.0 copy-done.20
  17.7 0.0 copy-done.21
  17.7 0.0 copy-done.22
  17.7 7.1 %conditional.1 = (f32[5,32,128]{2,1,0:T(8,128)}, f32[5,8,32,128]{3,2,1,0:T(8,128)}, f32[35,32,128]{2,1,0:T(8,128)S(1)}, f32[5,32,128]{2,1,0:T(8,128)S(1)}, f32[2...) conditional(s32[]{:T(128)} %bitcast.1, (f32[5,32,128]{2,1,0:T(8,128)S(1)}, ...), branch_computations={%region_0.0_spmd, %region_1.0_spmd, %region_2.0_spmd, %region_3.0_... | conditional | flops 100000000 | bytes 15449236 | solution.py:486
  17.9 1.3 %collective-permute-start.13 = (f32[5,32,128]{2,1,0:T(8,128)S(1)}, f32[5,32,128]{2,1,0:T(8,128)}, u32[]{:S(2)}, u32[]{:S(2)}) collective-permute-start(f32[5,32,128]{2,1,0:T(8,128)S(1)} %get-tuple-element.483), channel_id=1, source_target_pairs={{128,27},{3,240},{132,31},{7,244},{136,35},{11,248},{140,39},{15,2... | collective-permute-start | bytes 245768 | tf_op jit(solution)/shard_map/cond/branch_13_fun/ppermute | solution.py:455
  19.2 2.6 %matrices.29 = (f32[25,32,128]{2,1,0:T(8,128)S(1)}, f32[25,32,128]{2,1,0:T(8,128)S(1)}, f32[25,32,128]{2,1,0:T(8,128)S(1)}) custom-call(f32[5,1,5]{2,1,0:T(1,128)S(1)} %get-tuple-element.484.refs_0_, f32[1,5,5,8,32,128]{5,4,3,2,1,0:T(8,128)S(1)} %get-tuple-element.488.refs_1_.refs_4_), custom_call_target="tpu_custom_call" | custom-call | flops 60000000 | bytes 7500000 | tf_op jit(solution)/shard_map/cond/branch_13_fun/matrices/pallas_call | solution.py:456
  21.8 2.1 %residual.29 = (f32[5,8,32,128]{3,2,1,0:T(8,128)S(1)}, f32[35,32,128]{2,1,0:T(8,128)S(1)}, f32[5,32,128]{2,1,0:T(8,128)S(1)}) custom-call(f32[5,1,5]{2,1,0:T(1,128)S(1)} %get-tuple-element.484.refs_0_, f32[5,2,5]{2,1,0:T(2,128)S(1)} %get-tuple-element.485.refs_1_, f32[1,5,8,32,128]{4,3,2,1,0:T(8,128)S(1)} %get-tuple-element.486.refs_2_, ...), custom_call_target="tpu_custom_call" | custom-call | flops 40000000 | bytes 5000000 | tf_op jit(solution)/shard_map/cond/branch_13_fun/residual/pallas_call | solution.py:470
  23.9 0.0 copy-start.13
  23.9 0.0 collective-permute-done.13
  23.9 0.8 %copy-done.13 = f32[5,8,32,128]{3,2,1,0:T(8,128)} copy-done((f32[5,8,32,128]{3,2,1,0:T(8,128)}, f32[5,8,32,128]{3,2,1,0:T(8,128)S(1)}, u32[]{:S(2)}) %copy-start.13) | copy-done | bytes 655384 | tf_op jit(solution)/shard_map/cond
  24.7 0.0 copy-start.16
  24.7 0.0 copy-start.19
  24.7 0.8 %collective-permute-start.20 = (f32[35,32,128]{2,1,0:T(8,128)S(1)}, f32[35,32,128]{2,1,0:T(8,128)S(1)}, u32[]{:S(2)}, u32[]{:S(2)}) collective-permute-start(f32[35,32,128]{2,1,0:T(8,128)S(1)} %get-tuple-element.560.up), channel_id=1, source_target_pairs={{1,2},{5,6},{9,10},{13,14},{17,18},{21,22},{25,26},{29,30},{33,34}... | collective-permute-start | bytes 1720328 | tf_op jit(solution)/shard_map/ppermute | solution.py:491
  25.6 0.9 %first.1 = (f32[5,32,128]{2,1,0:T(8,128)S(1)}, f32[10,32,128]{2,1,0:T(8,128)S(1)}, f32[30,32,128]{2,1,0:T(8,128)S(1)}) custom-call(f32[5,32,128]{2,1,0:T(8,128)} %get-tuple-element.559.ghost.refs_1_, f32[35,32,128]{2,1,0:T(8,128)S(1)} %get-tuple-element.560.up, f32[5,32,128]{2,1,0:T(8,128)S(1)} %get-tuple-element.561.down, ...), custom_call_target="tpu_custom_call" | custom-call | tf_op jit(solution)/shard_map/first/pallas_call | solution.py:492
  26.5 0.7 %collective-permute-start.23 = (f32[30,32,128]{2,1,0:T(8,128)S(1)}, f32[30,32,128]{2,1,0:T(8,128)S(1)}, u32[]{:S(2)}, u32[]{:S(2)}) collective-permute-start(f32[30,32,128]{2,1,0:T(8,128)S(1)} %get-tuple-element.568), channel_id=1, source_target_pairs={{3,2},{7,6},{11,10},{15,14},{19,18},{23,22},{27,26},{31,30},{35,34... | collective-permute-start | bytes 1474568 | tf_op jit(solution)/shard_map/ppermute | solution.py:498
  27.2 9.5 %collective-permute-start.21 = (f32[5,32,128]{2,1,0:T(8,128)S(1)}, f32[5,32,128]{2,1,0:T(8,128)S(1)}, u32[]{:S(2)}, u32[]{:S(2)}) collective-permute-start(f32[5,32,128]{2,1,0:T(8,128)S(1)} %get-tuple-element.565), channel_id=1, source_target_pairs={{0,2},{4,6},{8,10},{12,14},{16,18},{20,22},{24,26},{28,30},{32,34}... | collective-permute-start | bytes 245768 | tf_op jit(solution)/shard_map/ppermute | solution.py:499
  36.7 2.0 %collective-permute-done.21.came = f32[5,32,128]{2,1,0:T(8,128)S(1)} collective-permute-done((f32[5,32,128]{2,1,0:T(8,128)S(1)}, f32[5,32,128]{2,1,0:T(8,128)S(1)}, u32[]{:S(2)}, u32[]{:S(2)}) %collective-permute-start.21) | collective-permute-done | bytes 81952 | tf_op jit(solution)/shard_map/ppermute | solution.py:499
  38.8 0.0 collective-permute-done.23.side_other
  38.8 0.0 collective-permute-done.20.up_other.refs_2_
  38.8 0.7 %collective-permute-start.24 = (f32[5,32,128]{2,1,0:T(8,128)S(1)}, f32[5,32,128]{2,1,0:T(8,128)S(1)}, u32[]{:S(2)}, u32[]{:S(2)}) collective-permute-start(f32[5,32,128]{2,1,0:T(8,128)S(1)} %get-tuple-element.570), channel_id=1, source_target_pairs={{2,1},{6,5},{10,9},{14,13},{18,17},{22,21},{26,25},{30,29},{34,33}... | collective-permute-start | bytes 245768 | tf_op jit(solution)/shard_map/ppermute | solution.py:508
  39.4 9.4 %collective-permute-start.22 = (f32[10,32,128]{2,1,0:T(8,128)S(1)}, f32[10,32,128]{2,1,0:T(8,128)S(1)}, u32[]{:S(2)}, u32[]{:S(2)}) collective-permute-start(f32[10,32,128]{2,1,0:T(8,128)S(1)} %get-tuple-element.566), channel_id=1, source_target_pairs={{0,1},{4,5},{8,9},{12,13},{16,17},{20,21},{24,25},{28,29},{32,33},... | collective-permute-start | bytes 491528 | tf_op jit(solution)/shard_map/ppermute | solution.py:501
  48.9 0.0 collective-permute-done.24.to_one.refs_6_
  48.9 0.7 %collective-permute-start.25 = (f32[10,32,128]{2,1,0:T(8,128)S(1)}, f32[10,32,128]{2,1,0:T(8,128)S(1)}, u32[]{:S(2)}, u32[]{:S(2)}) collective-permute-start(f32[10,32,128]{2,1,0:T(8,128)S(1)} %get-tuple-element.571), channel_id=1, source_target_pairs={{2,3},{6,7},{10,11},{14,15},{18,19},{22,23},{26,27},{30,31},{34,35... | collective-permute-start | bytes 491528 | tf_op jit(solution)/shard_map/ppermute | solution.py:510
  49.5 2.1 %collective-permute-done.22.came_side.refs_3_ = f32[10,32,128]{2,1,0:T(8,128)S(1)} collective-permute-done((f32[10,32,128]{2,1,0:T(8,128)S(1)}, f32[10,32,128]{2,1,0:T(8,128)S(1)}, u32[]{:S(2)}, u32[]{:S(2)}) %collective-permute-start.22) | collective-permute-done | bytes 163872 | tf_op jit(solution)/shard_map/ppermute | solution.py:501
  51.7 1.3 %collective-permute-start.26 = (f32[5,32,128]{2,1,0:T(8,128)S(1)}, f32[5,32,128]{2,1,0:T(8,128)S(1)}, u32[]{:S(2)}, u32[]{:S(2)}) collective-permute-start(f32[5,32,128]{2,1,0:T(8,128)S(1)} %lower.1), channel_id=1, source_target_pairs={{1,0},{5,4},{9,8},{13,12},{17,16},{21,20},{25,24},{29,28},{33,32},... | collective-permute-start | bytes 245768 | tf_op jit(solution)/shard_map/ppermute | solution.py:517
  53.0 5.0 %collective-permute-done.26.refs_5_ = f32[5,32,128]{2,1,0:T(8,128)S(1)} collective-permute-done((f32[5,32,128]{2,1,0:T(8,128)S(1)}, f32[5,32,128]{2,1,0:T(8,128)S(1)}, u32[]{:S(2)}, u32[]{:S(2)}) %collective-permute-start.26) | collective-permute-done | bytes 81952 | tf_op jit(solution)/shard_map/ppermute | solution.py:517
  58.0 0.0 collective-permute-done.25.refs_4_
  58.0 0.0 copy-done.16
  58.0 0.0 copy-done.19
  58.0 3.5 %last.1 = (f32[1,5,8,32,128]{4,3,2,1,0:T(8,128)}, f32[1,5,8,32,128]{4,3,2,1,0:T(8,128)}) custom-call(f32[5,1,5]{2,1,0:T(1,128)S(1)} %bitcast.21, f32[5,32,128]{2,1,0:T(8,128)} %get-tuple-element.559.ghost.refs_1_, f32[35,32,128]{2,1,0:T(8,128)S(1)} %collective-permute-done.20.up_other.refs_2_, f32[10,32,128]{2,1,0:T(8,128)S(1)} %collective-permute-done.22.came_side.refs_3_, ...), custom_call_target="tpu_custom_call" | custom-call | tf_op jit(solution)/shard_map/last/pallas_call | solution.py:519
  (2 shorter events, 0.0 us)
Async XLA Ops:
  1.8 10.8 %collective-permute-start.16 = (f32[5,40,128]{2,1,0:T(8,128)S(1)}, f32[5,40,128]{2,1,0:T(8,128)S(1)}, u32[]{:S(2)}, u32[]{:S(2)}) collective-permute-start(f32[5,40,128]{2,1,0:T(8,128)S(1)} %get-tuple-element.554), channel_id=1, source_target_pairs={{0,124},{4,0},{8,4},{12,8},{16,12},{20,16},{24,20},{28,24},{32,28}... | collective-permute-start | bytes 307208 | tf_op jit(solution)/shard_map/ppermute | solution.py:428
  8.4 4.1 %collective-permute-start.17 = (f32[5,32,128]{2,1,0:T(8,128)S(1)}, f32[5,32,128]{2,1,0:T(8,128)S(1)}, u32[]{:S(2)}, u32[]{:S(2)}) collective-permute-start(f32[5,32,128]{2,1,0:T(8,128)S(1)} %get-tuple-element.553.refs_1_), channel_id=1, source_target_pairs={{3,123},{128,248},{7,127},{132,252},{11,3},{136,128},{15,7},{140,1... | collective-permute-start | bytes 245768 | tf_op jit(solution)/shard_map/ppermute | solution.py:427
  9.1 8.6 %collective-permute-start.19 = (f32[5,32,128]{2,1,0:T(8,128)S(1)}, f32[5,32,128]{2,1,0:T(8,128)S(1)}, u32[]{:S(2)}, u32[]{:S(2)}) collective-permute-start(f32[5,32,128]{2,1,0:T(8,128)S(1)} %get-tuple-element.557.lowest), channel_id=1, source_target_pairs={{1,0},{2,1},{3,2},{5,4},{6,5},{7,6},{9,8},{10,9},{11,10},{13,12},{... | collective-permute-start | bytes 245768 | tf_op jit(solution)/shard_map/ppermute | solution.py:425
  10.4 2.2 %copy-start.17 = (s32[1024]{0:T(1024)S(1)}, s32[1024]{0:T(1024)}, u32[]{:S(2)}) copy-start(s32[1024]{0:T(1024)} %refs_0_.3) | copy-start | bytes 12292
  10.4 7.3 %copy-start.18 = (f32[1,5,8,32,128]{4,3,2,1,0:T(8,128)S(1)}, f32[1,5,8,32,128]{4,3,2,1,0:T(8,128)}, u32[]{:S(2)}) copy-start(f32[1,5,8,32,128]{4,3,2,1,0:T(8,128)} %refs_11_.1) | copy-start | bytes 1966084
  10.4 7.3 %copy-start.20 = (f32[1,5,8,32,128]{4,3,2,1,0:T(8,128)S(1)}, f32[1,5,8,32,128]{4,3,2,1,0:T(8,128)}, u32[]{:S(2)}) copy-start(f32[1,5,8,32,128]{4,3,2,1,0:T(8,128)} %param.23) | copy-start | bytes 1966084
  10.4 7.3 %copy-start.21 = (f32[1,5,5]{2,0,1:T(1,128)S(1)}, f32[1,5,5]{2,0,1:T(1,128)}, u32[]{:S(2)}) copy-start(f32[1,5,5]{2,0,1:T(1,128)} %param.25) | copy-start | bytes 304
  10.4 7.3 %copy-start.22 = (f32[1,2,5,5]{3,1,2,0:T(2,128)S(1)}, f32[1,2,5,5]{3,1,2,0:T(2,128)}, u32[]{:S(2)}) copy-start(f32[1,2,5,5]{3,1,2,0:T(2,128)} %param.26) | copy-start | bytes 604
  10.4 7.2 %collective-permute-start.18 = (f32[5,8,128]{2,1,0:T(8,128)S(1)}, f32[5,8,128]{2,1,0:T(8,128)S(1)}, u32[]{:S(2)}, u32[]{:S(2)}) collective-permute-start(f32[5,8,128]{2,1,0:T(8,128)S(1)} %get-tuple-element.558), channel_id=1, source_target_pairs={{0,4},{4,8},{8,12},{12,16},{16,20},{20,24},{24,28},{28,32},{32,36}... | collective-permute-start | bytes 61448 | tf_op jit(solution)/shard_map/ppermute | solution.py:426
  17.9 6.0 %collective-permute-start.13 = (f32[5,32,128]{2,1,0:T(8,128)S(1)}, f32[5,32,128]{2,1,0:T(8,128)}, u32[]{:S(2)}, u32[]{:S(2)}) collective-permute-start(f32[5,32,128]{2,1,0:T(8,128)S(1)} %get-tuple-element.483), channel_id=1, source_target_pairs={{128,27},{3,240},{132,31},{7,244},{136,35},{11,248},{140,39},{15,2... | collective-permute-start | bytes 245768 | tf_op jit(solution)/shard_map/cond/branch_13_fun/ppermute | solution.py:455
  23.9 0.8 %copy-start.13 = (f32[5,8,32,128]{3,2,1,0:T(8,128)}, f32[5,8,32,128]{3,2,1,0:T(8,128)S(1)}, u32[]{:S(2)}) copy-start(f32[5,8,32,128]{3,2,1,0:T(8,128)S(1)} %get-tuple-element.655) | copy-start | bytes 1966084 | tf_op jit(solution)/shard_map/cond
  24.7 33.3 %copy-start.16 = (f32[5,8,32,128]{3,2,1,0:T(8,128)S(1)}, f32[5,8,32,128]{3,2,1,0:T(8,128)}, u32[]{:S(2)}) copy-start(f32[5,8,32,128]{3,2,1,0:T(8,128)} %get-tuple-element.575.refs_9_) | copy-start | bytes 1966084
  24.7 33.3 %copy-start.19 = (f32[1,5,8,32,128]{4,3,2,1,0:T(8,128)S(1)}, f32[1,5,8,32,128]{4,3,2,1,0:T(8,128)}, u32[]{:S(2)}) copy-start(f32[1,5,8,32,128]{4,3,2,1,0:T(8,128)} %refs_11_.1) | copy-start | bytes 1966084
  24.7 14.0 %collective-permute-start.20 = (f32[35,32,128]{2,1,0:T(8,128)S(1)}, f32[35,32,128]{2,1,0:T(8,128)S(1)}, u32[]{:S(2)}, u32[]{:S(2)}) collective-permute-start(f32[35,32,128]{2,1,0:T(8,128)S(1)} %get-tuple-element.560.up), channel_id=1, source_target_pairs={{1,2},{5,6},{9,10},{13,14},{17,18},{21,22},{25,26},{29,30},{33,34}... | collective-permute-start | bytes 1720328 | tf_op jit(solution)/shard_map/ppermute | solution.py:491
  26.5 12.3 %collective-permute-start.23 = (f32[30,32,128]{2,1,0:T(8,128)S(1)}, f32[30,32,128]{2,1,0:T(8,128)S(1)}, u32[]{:S(2)}, u32[]{:S(2)}) collective-permute-start(f32[30,32,128]{2,1,0:T(8,128)S(1)} %get-tuple-element.568), channel_id=1, source_target_pairs={{3,2},{7,6},{11,10},{15,14},{19,18},{23,22},{27,26},{31,30},{35,34... | collective-permute-start | bytes 1474568 | tf_op jit(solution)/shard_map/ppermute | solution.py:498
  27.2 11.6 %collective-permute-start.21 = (f32[5,32,128]{2,1,0:T(8,128)S(1)}, f32[5,32,128]{2,1,0:T(8,128)S(1)}, u32[]{:S(2)}, u32[]{:S(2)}) collective-permute-start(f32[5,32,128]{2,1,0:T(8,128)S(1)} %get-tuple-element.565), channel_id=1, source_target_pairs={{0,2},{4,6},{8,10},{12,14},{16,18},{20,22},{24,26},{28,30},{32,34}... | collective-permute-start | bytes 245768 | tf_op jit(solution)/shard_map/ppermute | solution.py:499
  38.8 10.1 %collective-permute-start.24 = (f32[5,32,128]{2,1,0:T(8,128)S(1)}, f32[5,32,128]{2,1,0:T(8,128)S(1)}, u32[]{:S(2)}, u32[]{:S(2)}) collective-permute-start(f32[5,32,128]{2,1,0:T(8,128)S(1)} %get-tuple-element.570), channel_id=1, source_target_pairs={{2,1},{6,5},{10,9},{14,13},{18,17},{22,21},{26,25},{30,29},{34,33}... | collective-permute-start | bytes 245768 | tf_op jit(solution)/shard_map/ppermute | solution.py:508
  39.4 12.2 %collective-permute-start.22 = (f32[10,32,128]{2,1,0:T(8,128)S(1)}, f32[10,32,128]{2,1,0:T(8,128)S(1)}, u32[]{:S(2)}, u32[]{:S(2)}) collective-permute-start(f32[10,32,128]{2,1,0:T(8,128)S(1)} %get-tuple-element.566), channel_id=1, source_target_pairs={{0,1},{4,5},{8,9},{12,13},{16,17},{20,21},{24,25},{28,29},{32,33},... | collective-permute-start | bytes 491528 | tf_op jit(solution)/shard_map/ppermute | solution.py:501
  48.9 9.1 %collective-permute-start.25 = (f32[10,32,128]{2,1,0:T(8,128)S(1)}, f32[10,32,128]{2,1,0:T(8,128)S(1)}, u32[]{:S(2)}, u32[]{:S(2)}) collective-permute-start(f32[10,32,128]{2,1,0:T(8,128)S(1)} %get-tuple-element.571), channel_id=1, source_target_pairs={{2,3},{6,7},{10,11},{14,15},{18,19},{22,23},{26,27},{30,31},{34,35... | collective-permute-start | bytes 491528 | tf_op jit(solution)/shard_map/ppermute | solution.py:510
  51.7 6.3 %collective-permute-start.26 = (f32[5,32,128]{2,1,0:T(8,128)S(1)}, f32[5,32,128]{2,1,0:T(8,128)S(1)}, u32[]{:S(2)}, u32[]{:S(2)}) collective-permute-start(f32[5,32,128]{2,1,0:T(8,128)S(1)} %lower.1), channel_id=1, source_target_pairs={{1,0},{5,4},{9,8},{13,12},{17,16},{21,20},{25,24},{29,28},{33,32},... | collective-permute-start | bytes 245768 | tf_op jit(solution)/shard_map/ppermute | solution.py:517
